TPU v7x, 32 devices: a whole 2x2x4 slice. The times are simulated.
32 devices in a mesh: dp: 16 (over z, y, core), tensor: 2 (over x).
Axes of the slice: x: 2, y: 2, z: 4, core: 2. Of those that a mesh axis runs over, the one named last changes fastest.
Arguments:
- inputs: bfloat16 [8192, 2048], P(('dp', 'tensor')), may hold values from -6 to 6
- ln_gain: bfloat16 [2048], P('dp'), may hold values from 0.5 to 1.5
- ln_bias: bfloat16 [2048], P('dp'), may hold values from -3 to 3
- qkv_weight: bfloat16 [3, 2048, 2048], P(None, 'dp', 'tensor'), may hold values from -0.125 to 0.125
- out_weight: bfloat16 [2048, 2048], P('dp', 'tensor'), may hold values from -0.75 to 0.75
- fc1_weight: bfloat16 [2048, 8192], P('dp', 'tensor'), may hold values from -0.125 to 0.125
- fc2_weight: bfloat16 [2048, 8192], P('dp', 'tensor'), may hold values from -0.0625 to 0.0625
- cotangent: bfloat16 [8192, 2048], P(('dp', 'tensor')), may hold values from -6 to 6
- m_gain: float32 [2048], P('dp'), may hold values from -78 to 78
- v_gain: float32 [2048], P('dp'), may hold values from 250 to 2500
- m_bias: float32 [2048], P('dp'), may hold values from -78 to 78
- v_bias: float32 [2048], P('dp'), may hold values from 250 to 2500
- m_qkv: float32 [3, 2048, 2048], P(None, 'dp', 'tensor'), may hold values from -9 to 9
- v_qkv: float32 [3, 2048, 2048], P(None, 'dp', 'tensor'), may hold values from 3 to 30
- m_out: float32 [2048, 2048], P('dp', 'tensor'), may hold values from -18 to 18
- v_out: float32 [2048, 2048], P('dp', 'tensor'), may hold values from 10 to 100
- m_fc1: float32 [2048, 8192], P('dp', 'tensor'), may hold values from -24 to 24
- v_fc1: float32 [2048, 8192], P('dp', 'tensor'), may hold values from 25 to 250
- m_fc2: float32 [2048, 8192], P('dp', 'tensor'), may hold values from -48 to 48
- v_fc2: float32 [2048, 8192], P('dp', 'tensor'), may hold values from 80 to 800
Outputs:
- output: bfloat16 [8192, 2048], P(('dp', 'tensor'))
- input_grad: float32 [8192, 2048], P(('dp', 'tensor'))
- gain_grad: float32 [2048], P('dp')
- gain_update: float32 [2048], P('dp')
- gain_m: float32 [2048], P('dp')
- gain_v: float32 [2048], P('dp')
- bias_grad: float32 [2048], P('dp')
- bias_update: float32 [2048], P('dp')
- bias_m: float32 [2048], P('dp')
- bias_v: float32 [2048], P('dp')
- qkv_grad: float32 [3, 2048, 2048], P(None, 'dp', 'tensor')
- qkv_update: float32 [3, 2048, 2048], P(None, 'dp', 'tensor')
- qkv_m: float32 [3, 2048, 2048], P(None, 'dp', 'tensor')
- qkv_v: float32 [3, 2048, 2048], P(None, 'dp', 'tensor')
- out_grad: float32 [2048, 2048], P('dp', 'tensor')
- out_update: float32 [2048, 2048], P('dp', 'tensor')
- out_m: float32 [2048, 2048], P('dp', 'tensor')
- out_v: float32 [2048, 2048], P('dp', 'tensor')
- fc1_grad: float32 [2048, 8192], P('dp', 'tensor')
- fc1_update: float32 [2048, 8192], P('dp', 'tensor')
- fc1_m: float32 [2048, 8192], P('dp', 'tensor')
- fc1_v: float32 [2048, 8192], P('dp', 'tensor')
- fc2_grad: float32 [2048, 8192], P('dp', 'tensor')
- fc2_update: float32 [2048, 8192], P('dp', 'tensor')
- fc2_m: float32 [2048, 8192], P('dp', 'tensor')
- fc2_v: float32 [2048, 8192], P('dp', 'tensor')
All inputs are finite; a program needn't handle non-finite values.
Results may differ from a plain program's by a relative error of at most 0.0085.
The roundings to bfloat16 on the way count: a program that leaves them out, or rounds other values in their place, can miss the bound.
Values may be sent and summed in bfloat16 or wider, within the bound.
No kernel may reach another device: no remote copies, remote signals or barrier semaphores. Data moves between devices by JAX's collectives and lax.ppermute only.
A program may use at most 320 MiB of HBM per device.

v0:
```python
import jax
import jax.numpy as jnp
from jax import lax
from jax.sharding import PartitionSpec as P

HEAD = 64
ROT = 32
EPS_NORM = 1e-05
MASK_FILL = -1e30
BETA_ONE = 0.9
BETA_TWO = 0.95
ADAM_EPS = 1e-08
RATE = 0.02
DECAY = 0.1
STEP_COUNT = 10


def rope_angles(length):
    position = jnp.arange(length, dtype=jnp.float32)[:, None]
    inverse = 10000.0 ** (-(jnp.arange(ROT // 2, dtype=jnp.float32) * 2.0 / ROT))
    angles = position * inverse[None, :]
    return (jnp.cos(angles), jnp.sin(angles))


def rotate(tensor_in, cosine, sine_table):
    half_rot = ROT // 2
    first_half = tensor_in[..., :half_rot]
    second_half = tensor_in[..., half_rot:ROT]
    cos_wide = cosine[:, None, :]
    sin_wide = sine_table[:, None, :]
    return jnp.concatenate(
        [
            first_half * cos_wide - second_half * sin_wide,
            second_half * cos_wide + first_half * sin_wide,
            tensor_in[..., ROT:],
        ],
        axis=-1,
    )


def rotate_back(gradient, cosine, sine_table):
    half_rot = ROT // 2
    upper_part = gradient[..., :half_rot]
    lower_part = gradient[..., half_rot:ROT]
    cos_wide = cosine[:, None, :]
    sin_wide = sine_table[:, None, :]
    return jnp.concatenate(
        [
            upper_part * cos_wide + lower_part * sin_wide,
            lower_part * cos_wide - upper_part * sin_wide,
            gradient[..., ROT:],
        ],
        axis=-1,
    )


def gelu_tanh(values_in):
    return jax.nn.gelu(values_in, approximate=True)


def block_scores(query_rot, key_rot, first_row, block_rows, score_scale):
    scores = (
        jnp.einsum("qhd,khd->hqk", query_rot, key_rot, preferred_element_type=jnp.float32)
        * score_scale
    )
    row_index = first_row + jnp.arange(block_rows, dtype=jnp.int32)[:, None]
    col_index = jnp.arange(key_rot.shape[0], dtype=jnp.int32)[None, :]
    return (query_rot, jnp.where((col_index <= row_index)[None], scores, MASK_FILL))


def adamw(weight, gradient, moment, second):
    new_m = BETA_ONE * moment + (1.0 - BETA_ONE) * gradient
    new_v = BETA_TWO * second + (1.0 - BETA_TWO) * gradient * gradient
    m_hat = new_m / (1.0 - BETA_ONE**STEP_COUNT)
    v_hat = new_v / (1.0 - BETA_TWO**STEP_COUNT)
    update = -RATE * (m_hat / (jnp.sqrt(v_hat) + ADAM_EPS) + DECAY * weight.astype(jnp.float32))
    return (gradient, update, new_m, new_v)


def shards(
    inputs,
    ln_gain,
    ln_bias,
    qkv_weight,
    out_weight,
    fc1_weight,
    fc2_weight,
    cotangent,
    m_gain,
    v_gain,
    m_bias,
    v_bias,
    m_qkv,
    v_qkv,
    m_out,
    v_out,
    m_fc1,
    v_fc1,
    m_fc2,
    v_fc2,
):
    qkv_full, out_full, fc1_full, fc2_full, gain_full, bias_full = (
        lax.all_gather(qkv_weight, "dp", axis=1, tiled=True),
        lax.all_gather(out_weight, "dp", axis=0, tiled=True),
        lax.all_gather(fc1_weight, "dp", axis=0, tiled=True),
        lax.all_gather(fc2_weight, "dp", axis=0, tiled=True),
        lax.all_gather(ln_gain, "dp", axis=0, tiled=True),
        lax.all_gather(ln_bias, "dp", axis=0, tiled=True),
    )
    gain_wide = gain_full.astype(jnp.float32)
    bias_wide = bias_full.astype(jnp.float32)
    own_rows = inputs.astype(jnp.float32)
    centred = own_rows - jnp.mean(own_rows, axis=1, keepdims=True)
    inv_std = lax.rsqrt(jnp.mean(centred * centred, axis=1, keepdims=True) + EPS_NORM)
    normed = centred * inv_std
    hidden_own = (normed * gain_wide + bias_wide).astype(jnp.bfloat16)
    hidden = lax.all_gather(hidden_own, "tensor", axis=0, tiled=True)
    length = hidden.shape[0]
    width_local = qkv_full.shape[2]
    heads_local = width_local // HEAD
    score_scale = HEAD ** (-0.5)
    cosine, sine_table = rope_angles(length)
    projected = jnp.einsum("ld,cde->cle", hidden, qkv_full, preferred_element_type=jnp.float32)
    shaped = projected.reshape(3, length, heads_local, HEAD)
    query_rot = rotate(shaped[0], cosine, sine_table).astype(jnp.bfloat16)
    key_rot = rotate(shaped[1], cosine, sine_table).astype(jnp.bfloat16)
    values = shaped[2].astype(jnp.bfloat16)
    block_rows = min(512, length)
    count_blocks = length // block_rows
    starts = jnp.arange(count_blocks, dtype=jnp.int32) * block_rows

    def forward_block(first_row):
        query_block, scores = block_scores(query_rot, key_rot, first_row, block_rows, score_scale)
        row_max = jnp.max(scores, axis=2, keepdims=True)
        raw_exp = jnp.exp(scores - row_max)
        row_total = jnp.sum(raw_exp, axis=2, keepdims=True)
        softmax = (raw_exp / row_total).astype(jnp.bfloat16)
        ctx_block = jnp.einsum("hqk,khd->qhd", softmax, values, preferred_element_type=jnp.float32)
        return (ctx_block.astype(jnp.bfloat16), (row_max + jnp.log(row_total))[..., 0])

    contexts, log_totals = lax.map(forward_block, starts)
    context = contexts.reshape(length, width_local)
    attn_part = jnp.einsum("le,de->ld", context, out_full, preferred_element_type=jnp.float32)
    pre_act = jnp.dot(hidden, fc1_full, preferred_element_type=jnp.float32)
    activated = gelu_tanh(pre_act).astype(jnp.bfloat16)
    mlp_part = jnp.einsum("lf,df->ld", activated, fc2_full, preferred_element_type=jnp.float32)
    summed = lax.psum_scatter(attn_part + mlp_part, "tensor", scatter_dimension=0, tiled=True)
    output = (own_rows + summed).astype(jnp.bfloat16)
    qkv_back, out_back, fc1_back, fc2_back = (
        lax.all_gather(qkv_weight, "dp", axis=1, tiled=True),
        lax.all_gather(out_weight, "dp", axis=0, tiled=True),
        lax.all_gather(fc1_weight, "dp", axis=0, tiled=True),
        lax.all_gather(fc2_weight, "dp", axis=0, tiled=True),
    )
    cotan_full = lax.all_gather(cotangent, "tensor", axis=0, tiled=True)
    d_act = jnp.dot(cotan_full, fc2_back, preferred_element_type=jnp.float32)
    ignored, pull_back = jax.vjp(gelu_tanh, pre_act)
    d_pre = pull_back(d_act)[0].astype(jnp.bfloat16)
    d_hidden_mlp = jnp.einsum("lf,df->ld", d_pre, fc1_back, preferred_element_type=jnp.float32)
    d_context = jnp.dot(cotan_full, out_back, preferred_element_type=jnp.float32).astype(
        jnp.bfloat16
    )
    d_context = d_context.reshape(length, heads_local, HEAD)

    def backward_block(running, block_item):
        first_row, log_total = block_item
        d_keys, d_values = running
        query_block, scores = block_scores(query_rot, key_rot, first_row, block_rows, score_scale)
        softmax = jnp.exp(scores - log_total[:, :, None])
        d_soft = jnp.einsum("qhd,khd->hqk", d_context, values, preferred_element_type=jnp.float32)
        centre = jnp.sum(d_soft * softmax, axis=2, keepdims=True)
        d_scores = (softmax * (d_soft - centre)).astype(jnp.bfloat16)
        d_query = (
            jnp.einsum("hqk,khd->qhd", d_scores, key_rot, preferred_element_type=jnp.float32)
            * score_scale
        )
        d_keys = (
            d_keys
            + jnp.einsum("hqk,qhd->khd", d_scores, query_block, preferred_element_type=jnp.float32)
            * score_scale
        )
        d_values = d_values + jnp.einsum(
            "hqk,qhd->khd",
            softmax.astype(jnp.bfloat16),
            d_context,
            preferred_element_type=jnp.float32,
        )
        return ((d_keys, d_values), d_query)

    empty = jnp.zeros((length, heads_local, HEAD), jnp.float32)
    (d_keys, d_values), d_queries = lax.scan(backward_block, (empty, empty), (starts, log_totals))
    d_queries = d_queries.reshape(length, heads_local, HEAD)
    d_proj = (
        jnp.stack(
            [
                rotate_back(d_queries, cosine, sine_table),
                rotate_back(d_keys, cosine, sine_table),
                d_values,
            ]
        )
        .reshape(3, length, width_local)
        .astype(jnp.bfloat16)
    )
    qkv_part = jnp.einsum("ld,cle->cde", hidden, d_proj, preferred_element_type=jnp.float32)
    d_hidden_attn = jnp.einsum("cle,cde->ld", d_proj, qkv_back, preferred_element_type=jnp.float32)
    d_hidden = lax.psum_scatter(
        d_hidden_attn + d_hidden_mlp, "tensor", scatter_dimension=0, tiled=True
    )
    gain_part = jnp.sum(d_hidden * normed, axis=0)
    bias_part = jnp.sum(d_hidden, axis=0)
    scaled_grad = d_hidden * gain_wide
    input_grad = cotangent.astype(jnp.float32) + inv_std * (
        scaled_grad
        - jnp.mean(scaled_grad, axis=1, keepdims=True)
        - normed * jnp.mean(scaled_grad * normed, axis=1, keepdims=True)
    )
    fc2_part = jnp.einsum("ld,lf->df", cotan_full, activated, preferred_element_type=jnp.float32)
    fc1_part = jnp.einsum("ld,lf->df", hidden, d_pre, preferred_element_type=jnp.float32)
    out_part = jnp.einsum("ld,le->de", cotan_full, context, preferred_element_type=jnp.float32)
    qkv_grad, out_grad, fc1_grad, fc2_grad, gain_half, bias_half = (
        lax.psum_scatter(qkv_part, "dp", scatter_dimension=1, tiled=True),
        lax.psum_scatter(out_part, "dp", scatter_dimension=0, tiled=True),
        lax.psum_scatter(fc1_part, "dp", scatter_dimension=0, tiled=True),
        lax.psum_scatter(fc2_part, "dp", scatter_dimension=0, tiled=True),
        lax.psum_scatter(gain_part, "dp", scatter_dimension=0, tiled=True),
        lax.psum_scatter(bias_part, "dp", scatter_dimension=0, tiled=True),
    )
    gain_grad, bias_grad = lax.psum((gain_half, bias_half), "tensor")
    gain_res = adamw(ln_gain, gain_grad, m_gain, v_gain)
    bias_res = adamw(ln_bias, bias_grad, m_bias, v_bias)
    qkv_res = adamw(qkv_weight, qkv_grad, m_qkv, v_qkv)
    out_res = adamw(out_weight, out_grad, m_out, v_out)
    fc1_res = adamw(fc1_weight, fc1_grad, m_fc1, v_fc1)
    fc2_res = adamw(fc2_weight, fc2_grad, m_fc2, v_fc2)
    return (
        output,
        input_grad,
        gain_res[0],
        gain_res[1],
        gain_res[2],
        gain_res[3],
        bias_res[0],
        bias_res[1],
        bias_res[2],
        bias_res[3],
        qkv_res[0],
        qkv_res[1],
        qkv_res[2],
        qkv_res[3],
        out_res[0],
        out_res[1],
        out_res[2],
        out_res[3],
        fc1_res[0],
        fc1_res[1],
        fc1_res[2],
        fc1_res[3],
        fc2_res[0],
        fc2_res[1],
        fc2_res[2],
        fc2_res[3],
    )


def solution(mesh):
    return jax.shard_map(
        shards,
        mesh=mesh,
        in_specs=(
            P(("dp", "tensor"), None),
            P("dp"),
            P("dp"),
            P(None, "dp", "tensor"),
            P("dp", "tensor"),
            P("dp", "tensor"),
            P("dp", "tensor"),
            P(("dp", "tensor"), None),
            P("dp"),
            P("dp"),
            P("dp"),
            P("dp"),
            P(None, "dp", "tensor"),
            P(None, "dp", "tensor"),
            P("dp", "tensor"),
            P("dp", "tensor"),
            P("dp", "tensor"),
            P("dp", "tensor"),
            P("dp", "tensor"),
            P("dp", "tensor"),
        ),
        out_specs=(
            P(("dp", "tensor"), None),
            P(("dp", "tensor"), None),
            P("dp"),
            P("dp"),
            P("dp"),
            P("dp"),
            P("dp"),
            P("dp"),
            P("dp"),
            P("dp"),
            P(None, "dp", "tensor"),
            P(None, "dp", "tensor"),
            P(None, "dp", "tensor"),
            P(None, "dp", "tensor"),
            P("dp", "tensor"),
            P("dp", "tensor"),
            P("dp", "tensor"),
            P("dp", "tensor"),
            P("dp", "tensor"),
            P("dp", "tensor"),
            P("dp", "tensor"),
            P("dp", "tensor"),
            P("dp", "tensor"),
            P("dp", "tensor"),
            P("dp", "tensor"),
            P("dp", "tensor"),
        ),
        check_vma=False,
    )
```

profile of v0, /device:TPU:0, one launch (start us, length us, event | category | flops | bytes accessed | tf_op | source)
XLA Modules:
  0.0 1644.2 jit_solution(8891050419869749501)
XLA Ops:
  8.7 23.2 %all-gather = bf16[16,1,128]{2,1,0:T(2,128)(2,1)S(1)} all-gather(bf16[1,1,128]{2,1,0:T(2,128)(2,1)} %bitcast.78), channel_id=1, replica_groups=mesh['dp'=16,'tensor'=2] {'dp'}, dimensions={0}, use_global_device_ids=true | all-gather | bytes 4352 | tf_op jit(solution)/shard_map/all_gather | solution.py:107
  31.9 17.5 %all-gather.1 = bf16[16,1,128]{2,1,0:T(2,128)(2,1)S(1)} all-gather(bf16[1,1,128]{2,1,0:T(2,128)(2,1)} %bitcast.77), channel_id=1, replica_groups=mesh['dp'=16,'tensor'=2] {'dp'}, dimensions={0}, use_global_device_ids=true | all-gather | bytes 4352 | tf_op jit(solution)/shard_map/all_gather | solution.py:108
  50.7 1.4 fusion.20
  55.0 43.2 %all-gather.13.cloned.1.call-done = bf16[2048,1024]{1,0:T(8,128)(2,1)} async-done(((bf16[128,1024]{1,0:T(8,128)(2,1)}), bf16[2048,1024]{1,0:T(8,128)(2,1)}) %all-gather.13.cloned.1.call-update) | async-done | bytes 4194320 | tf_op jit(solution)/shard_map/all_gather | solution.py:104
  98.2 5.2 convolution_convert_fusion
  104.3 27.7 %all-gather.9.cloned.1.call-done = bf16[512,2048]{1,0:T(8,128)(2,1)} async-done(((bf16[256,2048]{1,0:T(8,128)(2,1)}), bf16[512,2048]{1,0:T(8,128)(2,1)}) %all-gather.9.cloned.1.call-update) | async-done | bytes 2097168 | tf_op jit(solution)/shard_map/all_gather | solution.py:117
  132.0 102.9 %all-gather.11.cloned.1.call-done = bf16[3,2048,1024]{2,1,0:T(8,128)(2,1)} async-done(((bf16[3,128,1024]{2,1,0:T(8,128)(2,1)}), bf16[3,2048,1024]{2,1,0:T(8,128)(2,1)}) %all-gather.11.cloned.1.call-update) | async-done | bytes 12582928 | tf_op jit(solution)/shard_map/all_gather | solution.py:103
  234.8 9.9 convolution_bitcast_fusion.3
  244.8 1.1 slice.104
  245.9 1.6 fusion.54
  247.5 2.9 copy.107
  250.4 1.8 copy.108
  252.2 2.2 slice.107
  254.4 2.1 slice.108
  256.5 2.3 copy.106
  258.8 1.6 subtract_convert_fusion.3
  260.6 7.4 fusion.55
  268.0 8.4 fusion
  277.1 7.6 fusion.33
  285.7 5.7 convolution_bitcast_fusion.2
  291.4 22.8 %multiply_reduce_fusion = (f32[16,512]{1,0:T(8,128)}, f32[16,512,512]{1,2,0:T(8,128)}) fusion(f32[16,512,512]{1,2,0:T(8,128)} %get-tuple-element.194, f32[16,512]{1,0:T(8,128)} %log_add_fusion, bf16[512,16,64]{0,2,1:T(8,128)(2,1)S(1)} %bitcast.62, bf16[512,16,64]{0,2,1:T(8,128)(2,1)} %bitcast.68), kind=kOutput, calls=%fused_computation.2 | convolution fusion | flops 549445632 | bytes 35717120 | tf_op jit(solution)/shard_map/while/body/eval_jaxpr/qhd,khd->hqk/dot_general | solution.py:170
  314.2 10.5 multiply_convert_fusion
  326.1 6.2 multiply_bitcast_fusion
  332.4 1.4 multiply_bitcast_fusion.1
  334.4 1.3 copy.114
  336.2 8.9 fusion.34
  345.2 1.3 copy.116
  346.5 11.4 fusion.37
  357.9 4.0 all-gather.17.cloned.1.call-done
  362.0 15.0 fusion.57
  376.9 112.1 %all-gather.15.cloned.1.call-done = bf16[2048,4096]{1,0:T(8,128)(2,1)} async-done(((bf16[128,4096]{1,0:T(8,128)(2,1)}), bf16[2048,4096]{1,0:T(8,128)(2,1)}) %all-gather.15.cloned.1.call-update) | async-done | bytes 16777232 | tf_op jit(solution)/shard_map/all_gather | solution.py:105
  489.0 20.6 %fusion.8 = (bf16[512,4096]{1,0:T(8,128)(2,1)S(1)}, f32[512,4096]{1,0:T(8,128)}) fusion(f32[512,4096]{1,0:T(8,128)} %fusion.57, bf16[512,2048]{1,0:T(8,128)(2,1)S(1)} %copy-done.10, bf16[2048,4096]{1,0:T(8,128)(2,1)} %all-gather.15.cloned.1.call-done), kind=kOutput, calls=%fused_computation.18 | convolution fusion | flops 8631877632 | bytes 39845888 | tf_op jit(solution)/shard_map/dot_general | solution.py:144
  509.7 2.1 copy-done.54
  511.7 14.8 bitcast_add_fusion
  526.7 6.8 fusion.56
  533.5 18.4 %convolution_add_fusion = f32[512,2048]{1,0:T(8,128)} fusion(f32[512,2048]{1,0:T(8,128)} %fusion.56, bf16[2048,4096]{1,0:T(8,128)(2,1)} %all-gather.17.cloned.1.call-done, f32[512,4096]{1,0:T(8,128)} %get-tuple-element.198), kind=kOutput, calls=%fused_computation.25 | convolution fusion | flops 8609857536 | bytes 33554432 | tf_op jit(solution)/shard_map/lf,df->ld/dot_general | solution.py:146
  552.0 13.6 convolution_bitcast_fusion.1
  565.7 17.8 %fusion.58 = f32[2048,4096]{1,0:T(8,128)} fusion(bf16[512,2048]{1,0:T(8,128)(2,1)S(1)} %copy-done.10, bf16[512,4096]{1,0:T(8,128)(2,1)} %copy-done.54), kind=kOutput, calls=%fused_computation.115 | convolution fusion | flops 8589934592 | bytes 39845888 | tf_op jit(solution)/shard_map/ld,lf->df/dot_general | solution.py:218
  583.6 1.5 copy-done.51
  585.1 19.7 %convolution_bitcast_fusion = f32[2048,4096]{1,0:T(8,128)} fusion(bf16[512,2048]{1,0:T(8,128)(2,1)S(1)} %copy-done.51, f32[512,4096]{1,0:T(8,128)} %get-tuple-element.198), kind=kOutput, calls=%fused_computation | convolution fusion | flops 8608808960 | bytes 44040192 | tf_op jit(solution)/shard_map/ld,lf->df/dot_general | solution.py:217
  604.9 1.1 copy-done.9
  606.0 1.2 copy.120
  607.7 1.6 copy.118
  609.3 3.1 copy.119
  614.1 1.4 add_multiply_fusion.3
  615.6 1.0 copy.130
  616.6 1.0 copy.131
  617.6 1.0 copy.132
  618.6 1.0 copy.129
  619.6 32.9 %reduce-scatter.9.cloned.1.call-done = f32[256,2048]{1,0:T(8,128)} async-done(((f32[512,2048]{1,0:T(8,128)}), f32[256,2048]{1,0:T(8,128)}) %reduce-scatter.9.cloned.1.call-update) | async-done | bytes 2097168 | tf_op jit(solution)/shard_map/reduce_scatter | solution.py:206
  652.5 2.7 fusion.25
  655.2 61.2 %all-reduce.2 = (f32[2048]{0:T(1024)S(1)}, f32[2048]{0:T(1024)S(1)}) all-reduce(f32[2048]{0:T(1024)S(1)} %get-tuple-element.149, f32[2048]{0:T(1024)S(1)} %get-tuple-element.152), channel_id=4, replica_groups=mesh['dp'=16,'tensor'=2] {'dp'}, use_global_device_ids=true, to_apply=%region_10.11.clone | all-reduce | flops 4096 | bytes 32768
  716.6 5.2 all-reduce.3
  722.9 5.5 fusion.24
  728.4 228.7 %reduce-scatter.11.cloned.1.call-done = f32[3,128,1024]{1,2,0:T(8,128)} async-done(((f32[3,2048,1024]{1,2,0:T(8,128)}), f32[3,128,1024]{1,2,0:T(8,128)}) %reduce-scatter.11.cloned.1.call-update) | async-done | bytes 1572880 | tf_op jit(solution)/shard_map/reduce_scatter | solution.py:221
  957.1 4.9 add_multiply_fusion.2
  962.0 3.0 copy.126
  965.0 1.6 copy.127
  966.7 1.6 copy.128
  968.3 1.6 copy.125
  969.9 323.9 %reduce-scatter.15.cloned.1.call-done = f32[128,4096]{1,0:T(8,128)} async-done(((f32[2048,4096]{1,0:T(8,128)}), f32[128,4096]{1,0:T(8,128)}) %reduce-scatter.15.cloned.1.call-update) | async-done | bytes 2097168 | tf_op jit(solution)/shard_map/reduce_scatter | solution.py:223
  1293.8 6.7 add_multiply_fusion.1
  1300.5 329.9 %reduce-scatter.17.cloned.1.call-done = f32[128,4096]{1,0:T(8,128)} async-done(((f32[2048,4096]{1,0:T(8,128)}), f32[128,4096]{1,0:T(8,128)}) %reduce-scatter.17.cloned.1.call-update) | async-done | bytes 2097168 | tf_op jit(solution)/shard_map/reduce_scatter | solution.py:224
  1630.4 6.7 add_multiply_fusion
  (169 shorter events, 13.6 us)
Async XLA Ops:
  7.2 42.2 %copy-start.1 = (bf16[256,2048]{1,0:T(8,128)(2,1)S(1)}, bf16[256,2048]{1,0:T(8,128)(2,1)}, u32[]{:S(2)}) copy-start(bf16[256,2048]{1,0:T(8,128)(2,1)} %param.20) | copy-start | bytes 3145732
  7.2 47.7 %all-gather.19.cloned.1.call-start = ((), (), s32[]{:S(2)}) async-start(), calls=%async_computation.12 | async-start | bytes 3145728 | tf_op jit(solution)/shard_map/all_gather | solution.py:155
  7.9 90.3 %all-gather.13.cloned.1.call-start = ((), (), s32[]{:S(2)}) async-start(), calls=%async_computation.8 | async-start | bytes 4456448 | tf_op jit(solution)/shard_map/all_gather | solution.py:104
  8.7 123.3 %all-gather.9.cloned.1.call-start = ((), (), s32[]{:S(2)}) async-start(), calls=%async_computation.6 | async-start | bytes 3145728 | tf_op jit(solution)/shard_map/all_gather | solution.py:117
  31.9 18.2 %copy-start.36 = (f32[16,1,128]{2,1,0:T(1,128)}, f32[16,1,128]{2,1,0:T(1,128)S(1)}, u32[]{:S(2)}) copy-start(f32[16,1,128]{2,1,0:T(1,128)S(1)} %convert_element_type.92) | copy-start | bytes 24580
  52.1 182.7 %all-gather.11.cloned.1.call-start = ((), (), s32[]{:S(2)}) async-start(), calls=%async_computation.7 | async-start | bytes 13369344 | tf_op jit(solution)/shard_map/all_gather | solution.py:103
  52.7 309.3 %all-gather.17.cloned.1.call-start = ((), (), s32[]{:S(2)}) async-start(), calls=%async_computation.10 | async-start | bytes 17825792 | tf_op jit(solution)/shard_map/all_gather | solution.py:106
  53.3 435.7 %all-gather.15.cloned.1.call-start = ((), (), s32[]{:S(2)}) async-start(), calls=%async_computation.9 | async-start | bytes 17825792 | tf_op jit(solution)/shard_map/all_gather | solution.py:105
  53.9 560.2 %reduce-scatter.13.cloned.1.call-start = ((), (), s32[]{:S(2)}) async-start(), calls=%async_computation.15 | async-start | bytes 8912896 | tf_op jit(solution)/shard_map/reduce_scatter | solution.py:222
  54.9 203.9 %copy-start.31 = (f32[512,16]{0,1:T(8,128)}, f32[512,16]{0,1:T(8,128)S(1)}, u32[]{:S(2)}) copy-start(f32[512,16]{0,1:T(8,128)S(1)} %get-tuple-element.191) | copy-start | bytes 98308
  54.9 203.9 %copy-start.33 = (f32[512,16]{0,1:T(8,128)}, f32[512,16]{0,1:T(8,128)S(1)}, u32[]{:S(2)}) copy-start(f32[512,16]{0,1:T(8,128)S(1)} %get-tuple-element.192) | copy-start | bytes 98308
  252.2 6.7 copy-start.4
  258.8 1.7 copy-start.11
  258.8 1.7 copy-start.13
  258.8 1.7 copy-start.35
  260.5 7.5 copy-start.17
  260.5 7.5 copy-start.19
  260.5 7.5 copy-start.21
  260.5 7.5 copy-start.23
  268.0 9.1 copy-start.6
  277.1 8.6 copy-start.50
  291.4 22.8 %slice-start = ((s8[16777216]{0:T(1024)(128)(4,1)}), s8[4194304]{0:T(1024)(128)(4,1)S(1)}, s32[]{:S(2)}) async-start(s8[16777216]{0:T(1024)(128)(4,1)} %bitcast.60), calls=%async_computation.18 | async-start | bytes 8388608
  291.4 22.8 %slice-start.1 = ((s8[16777216]{0:T(1024)(128)(4,1)}), s8[4194304]{0:T(1024)(128)(4,1)S(1)}, s32[]{:S(2)}) async-start(s8[16777216]{0:T(1024)(128)(4,1)} %bitcast.60), calls=%async_computation.19 | async-start | bytes 8388608
  291.4 22.8 %slice-start.2 = ((s8[16777216]{0:T(1024)(128)(4,1)}), s8[4194304]{0:T(1024)(128)(4,1)S(1)}, s32[]{:S(2)}) async-start(s8[16777216]{0:T(1024)(128)(4,1)} %bitcast.60), calls=%async_computation.20 | async-start | bytes 8388608
  291.4 22.8 %slice-start.3 = ((s8[16777216]{0:T(1024)(128)(4,1)}), s8[4194304]{0:T(1024)(128)(4,1)S(1)}, s32[]{:S(2)}) async-start(s8[16777216]{0:T(1024)(128)(4,1)} %bitcast.60), calls=%async_computation.21 | async-start | bytes 8388608
  324.8 7.5 copy-start.12
  324.8 7.5 copy-start.18
  324.8 7.5 copy-start.20
  324.9 327.6 %reduce-scatter.9.cloned.1.call-start = ((), (), s32[]{:S(2)}) async-start(), calls=%async_computation.13 | async-start | bytes 6291456 | tf_op jit(solution)/shard_map/reduce_scatter | solution.py:206
  326.1 6.3 copy-start
  332.3 1.5 copy-start.32
  332.3 1.5 copy-start.34
  334.4 1.9 copy-start.30
  336.2 10.3 copy-start.26
  345.2 1.3 copy-start.25
  357.9 131.1 %copy-start.10 = (bf16[512,2048]{1,0:T(8,128)(2,1)S(1)}, bf16[512,2048]{1,0:T(8,128)(2,1)}, u32[]{:S(2)}) copy-start(bf16[512,2048]{1,0:T(8,128)(2,1)} %all-gather.9.cloned.1.call-done) | copy-start | bytes 6291460
  509.7 2.1 copy-start.54
  526.6 196.3 %reduce-scatter.7.cloned.1.call-start = ((), (), s32[]{:S(2)}) async-start(), calls=%async_computation.11 | async-start | bytes 6291456 | tf_op jit(solution)/shard_map/reduce_scatter | solution.py:147
  552.0 405.2 %reduce-scatter.11.cloned.1.call-start = ((), (), s32[]{:S(2)}) async-start(), calls=%async_computation.14 | async-start | bytes 26738688 | tf_op jit(solution)/shard_map/reduce_scatter | solution.py:221
  565.6 728.1 %reduce-scatter.15.cloned.1.call-start = ((), (), s32[]{:S(2)}) async-start(), calls=%async_computation.16 | async-start | bytes 35651584 | tf_op jit(solution)/shard_map/reduce_scatter | solution.py:223
  583.5 1.6 copy-start.51
  583.5 1046.9 %reduce-scatter.17.cloned.1.call-start = ((), (), s32[]{:S(2)}) async-start(), calls=%async_computation.17 | async-start | bytes 35651584 | tf_op jit(solution)/shard_map/reduce_scatter | solution.py:224
  604.8 2.3 copy-start.27
  606.0 1.7 copy-start.16
  609.3 3.1 copy-start.28
  609.3 3.3 copy-start.29
  609.3 3.5 copy-start.53
  615.5 3.0 copy-start.15
  615.5 37.0 %copy-start.2 = (bf16[256,2048]{1,0:T(8,128)(2,1)S(1)}, bf16[256,2048]{1,0:T(8,128)(2,1)}, u32[]{:S(2)}) copy-start(bf16[256,2048]{1,0:T(8,128)(2,1)} %param.20) | copy-start | bytes 3145732
  615.6 37.0 %copy-start.37 = (f32[16,1,128]{2,1,0:T(1,128)S(1)}, f32[16,1,128]{2,1,0:T(1,128)}, u32[]{:S(2)}) copy-start(f32[16,1,128]{2,1,0:T(1,128)} %copy-done.36) | copy-start | bytes 24580
  615.6 36.9 %copy-start.39 = (f32[256]{0:T(256)S(1)}, f32[256]{0:T(256)}, u32[]{:S(2)}) copy-start(f32[256]{0:T(256)} %copy-done.38) | copy-start | bytes 3076
  615.6 36.9 %copy-start.41 = (f32[256]{0:T(256)S(1)}, f32[256]{0:T(256)}, u32[]{:S(2)}) copy-start(f32[256]{0:T(256)} %copy-done.40) | copy-start | bytes 3076
  618.6 103.2 %copy-start.42 = (bf16[128]{0:T(256)(128)(2,1)S(1)}, bf16[128]{0:T(256)(128)(2,1)}, u32[]{:S(2)}) copy-start(bf16[128]{0:T(256)(128)(2,1)} %param.22) | copy-start | bytes 772
  618.6 103.2 %copy-start.44 = (f32[128]{0:T(128)S(1)}, f32[128]{0:T(128)}, u32[]{:S(2)}) copy-start(f32[128]{0:T(128)} %param.30) | copy-start | bytes 1540
  618.6 103.2 %copy-start.45 = (f32[128]{0:T(128)S(1)}, f32[128]{0:T(128)}, u32[]{:S(2)}) copy-start(f32[128]{0:T(128)} %param.31) | copy-start | bytes 1540
  618.6 103.7 %copy-start.43 = (bf16[128]{0:T(256)(128)(2,1)S(1)}, bf16[128]{0:T(256)(128)(2,1)}, u32[]{:S(2)}) copy-start(bf16[128]{0:T(256)(128)(2,1)} %param.21) | copy-start | bytes 772
  618.6 103.7 %copy-start.46 = (f32[128]{0:T(128)S(1)}, f32[128]{0:T(128)}, u32[]{:S(2)}) copy-start(f32[128]{0:T(128)} %param.28) | copy-start | bytes 1540
  618.6 103.7 %copy-start.47 = (f32[128]{0:T(128)S(1)}, f32[128]{0:T(128)}, u32[]{:S(2)}) copy-start(f32[128]{0:T(128)} %param.29) | copy-start | bytes 1540
  652.5 70.4 %copy-start.3 = (f32[256,2048]{1,0:T(8,128)S(1)}, f32[256,2048]{1,0:T(8,128)}, u32[]{:S(2)}) copy-start(f32[256,2048]{1,0:T(8,128)} %reduce-scatter.9.cloned.1.call-done) | copy-start | bytes 6291460
  721.7 6.6 copy-start.48
  721.7 6.6 copy-start.49
  966.7 1.6 copy-start.5
  968.3 325.5 %copy-start.7 = (bf16[128,4096]{1,0:T(8,128)(2,1)S(1)}, bf16[128,4096]{1,0:T(8,128)(2,1)}, u32[]{:S(2)}) copy-start(bf16[128,4096]{1,0:T(8,128)(2,1)} %param.25) | copy-start | bytes 3145732
  969.9 660.5 %copy-start.8 = (bf16[128,4096]{1,0:T(8,128)(2,1)S(1)}, bf16[128,4096]{1,0:T(8,128)(2,1)}, u32[]{:S(2)}) copy-start(bf16[128,4096]{1,0:T(8,128)(2,1)} %param.26) | copy-start | bytes 3145732
  (7 other events, 6.7 us)
Sparse Core Ops, SparseCore 0:
  9.6 35.7 all-gather.18
  47.6 50.5 all-gather.12
  100.3 31.5 all-gather.8
  134.0 100.7 all-gather.10
  236.9 125.0 all-gather.16
  364.0 124.9 all-gather.14
  493.1 103.0 reduce-scatter.12
  598.4 54.0 reduce-scatter.8
  654.9 54.3 reduce-scatter.6
  713.2 243.8 reduce-scatter.10
  961.9 331.7 reduce-scatter.14
  1298.4 331.9 reduce-scatter.16
where the time goes:
time: 1650 us; the launch traced here: 1640 us
  waiting for transfers between devices  1210 us (73%)
  matrix products  213 us (13%)
  blocking collectives  107 us (6%)
  other arithmetic  53.9 us (3%)
  local copies, waits for them, and re-layouts  45.3 us (3%)
    reduce_scatter x1, waiting for transfers between devices, shards(): lax.psum_scatter(fc2_part, 'dp', scatter_dimension=0, tiled=True)  330 us
    reduce_scatter x1, waiting for transfers between devices, shards(): lax.psum_scatter(fc1_part, 'dp', scatter_dimension=0, tiled=True)  324 us
    reduce_scatter x1, waiting for transfers between devices, shards(): lax.psum_scatter(qkv_part, 'dp', scatter_dimension=1, tiled=True)  229 us
    all_gather x1, waiting for transfers between devices, shards(): lax.all_gather(fc1_weight, 'dp', axis=0, tiled=True)  112 us
    all_gather x1, waiting for transfers between devices, shards(): lax.all_gather(qkv_weight, 'dp', axis=1, tiled=True)  103 us
    unnamed x1, blocking collectives  61.2 us
    all_gather x1, waiting for transfers between devices, shards(): lax.all_gather(out_weight, 'dp', axis=0, tiled=True)  43.2 us
  transfers between devices with their start and end apart: 12, of which 9 were waited for; matrix products, arithmetic and copies ran while one was open for 18% of the time, Pallas kernels for 0%

commit v1 on v0

--- a/solution.py
+++ b/solution.py
@@ -13,6 +13,24 @@
 RATE = 0.02
 DECAY = 0.1
 STEP_COUNT = 10
+
+
+def collect(value, axis, dim):
+    ways, here, hop = (lax.axis_size(axis), lax.axis_index(axis), value.shape[dim])
+    shape = [n * ways if d == dim else n for d, n in enumerate(value.shape)]
+    full = lax.dynamic_update_slice_in_dim(
+        jnp.zeros(shape, value.dtype), value, here * hop, axis=dim
+    )
+    going_up = going_down = value
+    for far in range(1, ways // 2 + 1):
+        going_up = lax.ppermute(going_up, axis, [(d, (d + 1) % ways) for d in range(ways)])
+        full = lax.dynamic_update_slice_in_dim(full, going_up, (here - far) % ways * hop, axis=dim)
+        if 2 * far < ways:
+            going_down = lax.ppermute(going_down, axis, [(d, (d - 1) % ways) for d in range(ways)])
+            full = lax.dynamic_update_slice_in_dim(
+                full, going_down, (here + far) % ways * hop, axis=dim
+            )
+    return full
 
 
 def rope_angles(length):
@@ -102,7 +120,7 @@
     qkv_full, out_full, fc1_full, fc2_full, gain_full, bias_full = (
         lax.all_gather(qkv_weight, "dp", axis=1, tiled=True),
         lax.all_gather(out_weight, "dp", axis=0, tiled=True),
-        lax.all_gather(fc1_weight, "dp", axis=0, tiled=True),
+        collect(fc1_weight, "dp", 0),
         lax.all_gather(fc2_weight, "dp", axis=0, tiled=True),
         lax.all_gather(ln_gain, "dp", axis=0, tiled=True),
         lax.all_gather(ln_bias, "dp", axis=0, tiled=True),

time: 1650 us -> 1730 us (1.048)
  starting transfers between devices: 0.48 us -> 129 us
  waiting for transfers between devices: 1210 us -> 1130 us
  local copies, waits for them, and re-layouts: 45.3 us -> 75.2 us
    ppermute x0 -> x15, starting transfers between devices: none -> 128 us  [the longest x8 121 us: collect(): lax.ppermute(going_up, axis, [(d, (d + 1) % ways) for d in range(ways)])]
    all_gather x1, waiting for transfers between devices: 103 us -> 26.4 us  [shards(): lax.all_gather(qkv_weight, 'dp', axis=1, tiled=True)]
    ppermute x0 -> x15, waiting for transfers between devices: none -> 69.6 us  [the longest x8 69.5 us: collect(): lax.ppermute(going_up, axis, [(d, (d + 1) % ways) for d in range(ways)])]
    all_gather x1, waiting for transfers between devices: 43.2 us -> 0.01 us  [shards(): lax.all_gather(out_weight, 'dp', axis=0, tiled=True)]
    all_gather x1, waiting for transfers between devices: 27.7 us -> 0.01 us  [shards(): hidden = lax.all_gather(hidden_own, 'tensor', axis=0, tiled=True)]
    dynamic_update_slice x0 -> x16, local copies, waits for them, and re-layouts: none -> 19.6 us  [the longest x8 9.73 us: collect(): lax.dynamic_update_slice_in_dim(full, going_up, (here - far) % ways * hop...]
    all_gather x1, waiting for transfers between devices: 112 us -> 94.4 us  [shards(): lax.all_gather(fc1_weight, 'dp', axis=0, tiled=True)]
  transfers between devices with their start and end apart: 12 -> 27, of which waited for: 9 -> 15; matrix products, arithmetic and copies ran while one was open for 18% -> 19% of each run, Pallas kernels for 0% -> 0%
where the time goes in v1:
time: 1730 us; the launch traced here: 1720 us
  waiting for transfers between devices  1130 us (65%)
  matrix products  209 us (12%)
  starting transfers between devices  129 us (7%)
  blocking collectives  107 us (6%)
  local copies, waits for them, and re-layouts  75.2 us (4%)
  other arithmetic  57.2 us (3%)
    reduce_scatter x1, waiting for transfers between devices, shards(): lax.psum_scatter(fc2_part, 'dp', scatter_dimension=0, tiled=True)  330 us
    reduce_scatter x1, waiting for transfers between devices, shards(): lax.psum_scatter(fc1_part, 'dp', scatter_dimension=0, tiled=True)  322 us
    reduce_scatter x1, waiting for transfers between devices, shards(): lax.psum_scatter(qkv_part, 'dp', scatter_dimension=1, tiled=True)  229 us
    ppermute x8, starting transfers between devices, collect(): lax.ppermute(going_up, axis, [(d, (d + 1) % ways) for d in range(ways)])  121 us
    all_gather x1, waiting for transfers between devices, shards(): lax.all_gather(fc1_weight, 'dp', axis=0, tiled=True)  94.4 us
    ppermute x8, waiting for transfers between devices, collect(): lax.ppermute(going_up, axis, [(d, (d + 1) % ways) for d in range(ways)])  69.5 us
    unnamed x1, blocking collectives  61.2 us
    reduce_scatter x1, waiting for transfers between devices, shards(): lax.psum_scatter(d_hidden_attn + d_hidden_mlp, 'tensor', scatter_dimensio...  47.7 us
  transfers between devices with their start and end apart: 27, of which 15 were waited for; matrix products, arithmetic and copies ran while one was open for 19% of the time, Pallas kernels for 0%

profile of v1, /device:TPU:0, one launch (start us, length us, event | category | flops | bytes accessed | tf_op | source)
XLA Modules:
  0.0 1724.8 jit_solution(17952505552094620324)
XLA Ops:
  8.7 23.2 %all-gather.1 = bf16[16,1,128]{2,1,0:T(2,128)(2,1)S(1)} all-gather(bf16[1,1,128]{2,1,0:T(2,128)(2,1)} %bitcast.78), channel_id=1, replica_groups=mesh['dp'=16,'tensor'=2] {'dp'}, dimensions={0}, use_global_device_ids=true | all-gather | bytes 4352 | tf_op jit(solution)/shard_map/all_gather | solution.py:126
  31.9 17.5 %all-gather = bf16[16,1,128]{2,1,0:T(2,128)(2,1)S(1)} all-gather(bf16[1,1,128]{2,1,0:T(2,128)(2,1)} %bitcast.77), channel_id=1, replica_groups=mesh['dp'=16,'tensor'=2] {'dp'}, dimensions={0}, use_global_device_ids=true | all-gather | bytes 4352 | tf_op jit(solution)/shard_map/all_gather | solution.py:125
  55.5 4.1 collective-permute-start.1
  59.6 21.0 %collective-permute-done = bf16[128,4096]{1,0:T(8,128)(2,1)S(1)} collective-permute-done((bf16[128,4096]{1,0:T(8,128)(2,1)S(1)}, bf16[128,4096]{1,0:T(8,128)(2,1)S(1)}, u32[]{:S(2)}, u32[]{:S(2)}) %collective-permute-start) | collective-permute-done | bytes 1048608 | tf_op jit(solution)/shard_map/ppermute | solution.py:26
  81.5 3.6 collective-permute-start.3
  85.1 21.2 %collective-permute-done.2 = bf16[128,4096]{1,0:T(8,128)(2,1)} collective-permute-done((bf16[128,4096]{1,0:T(8,128)(2,1)S(1)}, bf16[128,4096]{1,0:T(8,128)(2,1)}, u32[]{:S(2)}, u32[]{:S(2)}) %collective-permute-start.2) | collective-permute-done | bytes 1048608 | tf_op jit(solution)/shard_map/ppermute | solution.py:26
  106.3 10.1 collective-permute-start.4
  118.1 6.1 broadcast_in_dim.79
  125.2 5.4 collective-permute-done.4
  130.6 10.8 collective-permute-start.6
  142.5 2.4 constant_dynamic-update-slice_fusion.13
  144.9 2.3 constant_dynamic-update-slice_fusion.12
  148.7 17.2 collective-permute-start.8
  169.0 2.1 collective-permute-done.8
  171.1 28.6 %collective-permute-start.10 = (bf16[128,4096]{1,0:T(8,128)(2,1)S(1)}, bf16[128,4096]{1,0:T(8,128)(2,1)S(1)}, u32[]{:S(2)}, u32[]{:S(2)}) collective-permute-start(bf16[128,4096]{1,0:T(8,128)(2,1)S(1)} %collective-permute-done.8), channel_id=1, source_target_pairs={{0,2},{2,4},{4,6},{6,8},{8,10},{10,12},{12,14},{14,16},{16,18},{18... | collective-permute-start | bytes 3145736 | tf_op jit(solution)/shard_map/ppermute | solution.py:26
  202.9 11.7 collective-permute-done.10
  214.6 14.9 collective-permute-start.12
  232.8 6.7 collective-permute-done.12
  239.5 37.8 %collective-permute-start.14 = (bf16[128,4096]{1,0:T(8,128)(2,1)S(1)}, bf16[128,4096]{1,0:T(8,128)(2,1)S(1)}, u32[]{:S(2)}, u32[]{:S(2)}) collective-permute-start(bf16[128,4096]{1,0:T(8,128)(2,1)S(1)} %collective-permute-done.12), channel_id=1, source_target_pairs={{0,2},{2,4},{4,6},{6,8},{8,10},{10,12},{12,14},{14,16},{16,18},{18... | collective-permute-start | bytes 3145736 | tf_op jit(solution)/shard_map/ppermute | solution.py:26
  279.4 6.3 convolution_convert_fusion
  288.7 26.4 %all-gather.11.cloned.1.call-done = bf16[3,2048,1024]{2,1,0:T(8,128)(2,1)} async-done(((bf16[3,128,1024]{2,1,0:T(8,128)(2,1)}), bf16[3,2048,1024]{2,1,0:T(8,128)(2,1)}) %all-gather.11.cloned.1.call-update) | async-done | bytes 12582928 | tf_op jit(solution)/shard_map/all_gather | solution.py:121
  315.0 9.9 convolution_bitcast_fusion.3
  327.7 2.9 copy.108
  330.6 2.1 slice.107
  334.5 2.2 slice.108
  336.7 2.3 copy.106
  340.7 8.6 fusion.55
  349.3 8.4 fusion
  358.4 7.6 fusion.33
  367.0 5.6 convolution_bitcast_fusion.2
  372.6 14.7 multiply_reduce_fusion
  389.6 10.5 multiply_convert_fusion
  400.9 8.7 fusion.34
  410.2 4.9 multiply_bitcast_fusion.1
  415.2 6.3 multiply_bitcast_fusion
  424.9 11.4 fusion.37
  436.4 6.2 all-gather.15.cloned.1.call-done
  442.6 12.5 fusion.57
  455.1 20.2 %fusion.8 = (bf16[512,4096]{1,0:T(8,128)(2,1)}, f32[512,4096]{1,0:T(8,128)}) fusion(f32[512,4096]{1,0:T(8,128)S(1)} %fusion.57, bf16[512,2048]{1,0:T(8,128)(2,1)S(1)} %copy-done.10, bf16[2048,4096]{1,0:T(8,128)(2,1)} %constant_dynamic-update-slice_fusion), kind=kOutput, calls=%fused_computation.18 | convolution fusion | flops 8631877632 | bytes 39845888 | tf_op jit(solution)/shard_map/dot_general | solution.py:162
  475.3 94.4 %all-gather.19.cloned.1.call-done = bf16[2048,4096]{1,0:T(8,128)(2,1)} async-done(((bf16[128,4096]{1,0:T(8,128)(2,1)}), bf16[2048,4096]{1,0:T(8,128)(2,1)}) %all-gather.19.cloned.1.call-update) | async-done | bytes 16777232 | tf_op jit(solution)/shard_map/all_gather | solution.py:170
  569.7 15.9 bitcast_add_fusion
  585.6 7.4 fusion.56
  593.1 18.6 %convolution_add_fusion = f32[512,2048]{1,0:T(8,128)} fusion(f32[512,2048]{1,0:T(8,128)} %fusion.56, bf16[2048,4096]{1,0:T(8,128)(2,1)} %all-gather.15.cloned.1.call-done, f32[512,4096]{1,0:T(8,128)} %get-tuple-element.198), kind=kOutput, calls=%fused_computation.25 | convolution fusion | flops 8609857536 | bytes 33554432 | tf_op jit(solution)/shard_map/lf,df->ld/dot_general | solution.py:164
  611.8 13.6 convolution_bitcast_fusion.1
  625.4 17.9 %fusion.58 = f32[2048,4096]{1,0:T(8,128)} fusion(bf16[512,2048]{1,0:T(8,128)(2,1)S(1)} %copy-done.10, bf16[512,4096]{1,0:T(8,128)(2,1)} %get-tuple-element.197), kind=kOutput, calls=%fused_computation.131 | convolution fusion | flops 8589934592 | bytes 39845888 | tf_op jit(solution)/shard_map/ld,lf->df/dot_general | solution.py:236
  644.9 19.3 %convolution_bitcast_fusion = f32[2048,4096]{1,0:T(8,128)} fusion(bf16[512,2048]{1,0:T(8,128)(2,1)S(1)} %copy-done.51, f32[512,4096]{1,0:T(8,128)} %get-tuple-element.198), kind=kOutput, calls=%fused_computation | convolution fusion | flops 8608808960 | bytes 44040192 | tf_op jit(solution)/shard_map/ld,lf->df/dot_general | solution.py:235
  668.4 3.1 copy.119
  673.1 3.6 reduce-scatter.13.cloned.1.call-done
  676.8 2.5 add_multiply_fusion.3
  679.2 2.0 copy.130
  681.3 2.1 copy.131
  685.4 47.7 %reduce-scatter.9.cloned.1.call-done = f32[256,2048]{1,0:T(8,128)} async-done(((f32[512,2048]{1,0:T(8,128)}), f32[256,2048]{1,0:T(8,128)}) %reduce-scatter.9.cloned.1.call-update) | async-done | bytes 2097168 | tf_op jit(solution)/shard_map/reduce_scatter | solution.py:224
  733.2 2.7 fusion.25
  735.9 61.2 %all-reduce.2 = (f32[2048]{0:T(1024)S(1)}, f32[2048]{0:T(1024)S(1)}) all-reduce(f32[2048]{0:T(1024)S(1)} %get-tuple-element.149, f32[2048]{0:T(1024)S(1)} %get-tuple-element.152), channel_id=4, replica_groups=mesh['dp'=16,'tensor'=2] {'dp'}, use_global_device_ids=true, to_apply=%region_10.11.clone | all-reduce | flops 4096 | bytes 32768
  797.2 5.2 all-reduce.3
  803.5 5.5 fusion.24
  809.0 228.8 %reduce-scatter.11.cloned.1.call-done = f32[3,128,1024]{1,2,0:T(8,128)} async-done(((f32[3,2048,1024]{1,2,0:T(8,128)}), f32[3,128,1024]{1,2,0:T(8,128)}) %reduce-scatter.11.cloned.1.call-update) | async-done | bytes 1572880 | tf_op jit(solution)/shard_map/reduce_scatter | solution.py:239
  1037.8 5.4 add_multiply_fusion.2
  1044.8 3.1 copy.127
  1047.9 3.1 copy.128
  1052.7 321.8 %reduce-scatter.15.cloned.1.call-done = f32[128,4096]{1,0:T(8,128)} async-done(((f32[2048,4096]{1,0:T(8,128)}), f32[128,4096]{1,0:T(8,128)}) %reduce-scatter.15.cloned.1.call-update) | async-done | bytes 2097168 | tf_op jit(solution)/shard_map/reduce_scatter | solution.py:241
  1374.5 6.7 add_multiply_fusion.1
  1381.2 329.8 %reduce-scatter.17.cloned.1.call-done = f32[128,4096]{1,0:T(8,128)} async-done(((f32[2048,4096]{1,0:T(8,128)}), f32[128,4096]{1,0:T(8,128)}) %reduce-scatter.17.cloned.1.call-update) | async-done | bytes 2097168 | tf_op jit(solution)/shard_map/reduce_scatter | solution.py:242
  1711.0 6.7 add_multiply_fusion
  (214 shorter events, 56.5 us)
Async XLA Ops:
  7.2 43.7 %copy-start = (bf16[256,2048]{1,0:T(8,128)(2,1)S(1)}, bf16[256,2048]{1,0:T(8,128)(2,1)}, u32[]{:S(2)}) copy-start(bf16[256,2048]{1,0:T(8,128)(2,1)} %param.20) | copy-start | bytes 3145732
  7.2 272.2 %all-gather.17.cloned.1.call-start = ((), (), s32[]{:S(2)}) async-start(), calls=%async_computation.11 | async-start | bytes 3145728 | tf_op jit(solution)/shard_map/all_gather | solution.py:173
  7.9 271.5 %all-gather.13.cloned.1.call-start = ((), (), s32[]{:S(2)}) async-start(), calls=%async_computation.8 | async-start | bytes 4456448 | tf_op jit(solution)/shard_map/all_gather | solution.py:122
  8.7 280.0 %all-gather.9.cloned.1.call-start = ((), (), s32[]{:S(2)}) async-start(), calls=%async_computation.6 | async-start | bytes 3145728 | tf_op jit(solution)/shard_map/all_gather | solution.py:135
  53.3 261.7 %all-gather.11.cloned.1.call-start = ((), (), s32[]{:S(2)}) async-start(), calls=%async_computation.7 | async-start | bytes 13369344 | tf_op jit(solution)/shard_map/all_gather | solution.py:121
  53.9 388.7 %all-gather.15.cloned.1.call-start = ((), (), s32[]{:S(2)}) async-start(), calls=%async_computation.9 | async-start | bytes 17825792 | tf_op jit(solution)/shard_map/all_gather | solution.py:124
  54.5 515.2 %all-gather.19.cloned.1.call-start = ((), (), s32[]{:S(2)}) async-start(), calls=%async_computation.12 | async-start | bytes 17825792 | tf_op jit(solution)/shard_map/all_gather | solution.py:170
  55.1 621.7 %reduce-scatter.13.cloned.1.call-start = ((), (), s32[]{:S(2)}) async-start(), calls=%async_computation.15 | async-start | bytes 8912896 | tf_op jit(solution)/shard_map/reduce_scatter | solution.py:240
  55.1 25.5 %collective-permute-start = (bf16[128,4096]{1,0:T(8,128)(2,1)S(1)}, bf16[128,4096]{1,0:T(8,128)(2,1)S(1)}, u32[]{:S(2)}, u32[]{:S(2)}) collective-permute-start(bf16[128,4096]{1,0:T(8,128)(2,1)S(1)} %copy-done.2), channel_id=1, source_target_pairs={{0,2},{2,4},{4,6},{6,8},{8,10},{10,12},{12,14},{14,16},{16,18},{18... | collective-permute-start | bytes 3145736 | tf_op jit(solution)/shard_map/ppermute | solution.py:26
  55.5 26.0 %collective-permute-start.1 = (bf16[128,4096]{1,0:T(8,128)(2,1)S(1)}, bf16[128,4096]{1,0:T(8,128)(2,1)}, u32[]{:S(2)}, u32[]{:S(2)}) collective-permute-start(bf16[128,4096]{1,0:T(8,128)(2,1)S(1)} %copy-done.2), channel_id=1, source_target_pairs={{0,30},{2,0},{4,2},{6,4},{8,6},{10,8},{12,10},{14,12},{16,14},{18,... | collective-permute-start | bytes 3145736 | tf_op jit(solution)/shard_map/ppermute | solution.py:29
  80.7 25.6 %collective-permute-start.2 = (bf16[128,4096]{1,0:T(8,128)(2,1)S(1)}, bf16[128,4096]{1,0:T(8,128)(2,1)}, u32[]{:S(2)}, u32[]{:S(2)}) collective-permute-start(bf16[128,4096]{1,0:T(8,128)(2,1)S(1)} %collective-permute-done), channel_id=1, source_target_pairs={{0,2},{2,4},{4,6},{6,8},{8,10},{10,12},{12,14},{14,16},{16,18},{18... | collective-permute-start | bytes 3145736 | tf_op jit(solution)/shard_map/ppermute | solution.py:26
  81.5 35.7 %collective-permute-start.3 = (bf16[128,4096]{1,0:T(8,128)(2,1)}, bf16[128,4096]{1,0:T(8,128)(2,1)S(1)}, u32[]{:S(2)}, u32[]{:S(2)}) collective-permute-start(bf16[128,4096]{1,0:T(8,128)(2,1)} %collective-permute-done.1), channel_id=1, source_target_pairs={{0,30},{2,0},{4,2},{6,4},{8,6},{10,8},{12,10},{14,12},{16,14},{18,... | collective-permute-start | bytes 3145736 | tf_op jit(solution)/shard_map/ppermute | solution.py:29
  106.3 24.3 %collective-permute-start.4 = (bf16[128,4096]{1,0:T(8,128)(2,1)}, bf16[128,4096]{1,0:T(8,128)(2,1)S(1)}, u32[]{:S(2)}, u32[]{:S(2)}) collective-permute-start(bf16[128,4096]{1,0:T(8,128)(2,1)} %collective-permute-done.2), channel_id=1, source_target_pairs={{0,2},{2,4},{4,6},{6,8},{8,10},{10,12},{12,14},{14,16},{16,18},{18... | collective-permute-start | bytes 3145736 | tf_op jit(solution)/shard_map/ppermute | solution.py:26
  117.3 25.2 %collective-permute-start.5 = (bf16[128,4096]{1,0:T(8,128)(2,1)S(1)}, bf16[128,4096]{1,0:T(8,128)(2,1)S(1)}, u32[]{:S(2)}, u32[]{:S(2)}) collective-permute-start(bf16[128,4096]{1,0:T(8,128)(2,1)S(1)} %collective-permute-done.3), channel_id=1, source_target_pairs={{0,30},{2,0},{4,2},{6,4},{8,6},{10,8},{12,10},{14,12},{16,14},{18,... | collective-permute-start | bytes 3145736 | tf_op jit(solution)/shard_map/ppermute | solution.py:29
  118.1 23.4 %copy-start.26 = (bf16[128,4096]{1,0:T(8,128)(2,1)S(1)}, bf16[128,4096]{1,0:T(8,128)(2,1)}, u32[]{:S(2)}) copy-start(bf16[128,4096]{1,0:T(8,128)(2,1)} %copy-done.25) | copy-start | bytes 3145732
  130.6 18.1 %collective-permute-start.6 = (bf16[128,4096]{1,0:T(8,128)(2,1)S(1)}, bf16[128,4096]{1,0:T(8,128)(2,1)S(1)}, u32[]{:S(2)}, u32[]{:S(2)}) collective-permute-start(bf16[128,4096]{1,0:T(8,128)(2,1)S(1)} %collective-permute-done.4), channel_id=1, source_target_pairs={{0,2},{2,4},{4,6},{6,8},{8,10},{10,12},{12,14},{14,16},{16,18},{18... | collective-permute-start | bytes 3145736 | tf_op jit(solution)/shard_map/ppermute | solution.py:26
  142.5 24.4 %collective-permute-start.7 = (bf16[128,4096]{1,0:T(8,128)(2,1)S(1)}, bf16[128,4096]{1,0:T(8,128)(2,1)S(1)}, u32[]{:S(2)}, u32[]{:S(2)}) collective-permute-start(bf16[128,4096]{1,0:T(8,128)(2,1)S(1)} %collective-permute-done.5), channel_id=1, source_target_pairs={{0,30},{2,0},{4,2},{6,4},{8,6},{10,8},{12,10},{14,12},{16,14},{18,... | collective-permute-start | bytes 3145736 | tf_op jit(solution)/shard_map/ppermute | solution.py:29
  148.7 22.4 %collective-permute-start.8 = (bf16[128,4096]{1,0:T(8,128)(2,1)S(1)}, bf16[128,4096]{1,0:T(8,128)(2,1)S(1)}, u32[]{:S(2)}, u32[]{:S(2)}) collective-permute-start(bf16[128,4096]{1,0:T(8,128)(2,1)S(1)} %collective-permute-done.6), channel_id=1, source_target_pairs={{0,2},{2,4},{4,6},{6,8},{8,10},{10,12},{12,14},{14,16},{16,18},{18... | collective-permute-start | bytes 3145736 | tf_op jit(solution)/shard_map/ppermute | solution.py:26
  166.9 33.8 %collective-permute-start.9 = (bf16[128,4096]{1,0:T(8,128)(2,1)S(1)}, bf16[128,4096]{1,0:T(8,128)(2,1)S(1)}, u32[]{:S(2)}, u32[]{:S(2)}) collective-permute-start(bf16[128,4096]{1,0:T(8,128)(2,1)S(1)} %collective-permute-done.7), channel_id=1, source_target_pairs={{0,30},{2,0},{4,2},{6,4},{8,6},{10,8},{12,10},{14,12},{16,14},{18,... | collective-permute-start | bytes 3145736 | tf_op jit(solution)/shard_map/ppermute | solution.py:29
  171.1 43.5 %collective-permute-start.10 = (bf16[128,4096]{1,0:T(8,128)(2,1)S(1)}, bf16[128,4096]{1,0:T(8,128)(2,1)S(1)}, u32[]{:S(2)}, u32[]{:S(2)}) collective-permute-start(bf16[128,4096]{1,0:T(8,128)(2,1)S(1)} %collective-permute-done.8), channel_id=1, source_target_pairs={{0,2},{2,4},{4,6},{6,8},{8,10},{10,12},{12,14},{14,16},{16,18},{18... | collective-permute-start | bytes 3145736 | tf_op jit(solution)/shard_map/ppermute | solution.py:26
  200.7 29.9 %collective-permute-start.11 = (bf16[128,4096]{1,0:T(8,128)(2,1)S(1)}, bf16[128,4096]{1,0:T(8,128)(2,1)S(1)}, u32[]{:S(2)}, u32[]{:S(2)}) collective-permute-start(bf16[128,4096]{1,0:T(8,128)(2,1)S(1)} %collective-permute-done.9), channel_id=1, source_target_pairs={{0,30},{2,0},{4,2},{6,4},{8,6},{10,8},{12,10},{14,12},{16,14},{18,... | collective-permute-start | bytes 3145736 | tf_op jit(solution)/shard_map/ppermute | solution.py:29
  214.6 24.8 %collective-permute-start.12 = (bf16[128,4096]{1,0:T(8,128)(2,1)S(1)}, bf16[128,4096]{1,0:T(8,128)(2,1)S(1)}, u32[]{:S(2)}, u32[]{:S(2)}) collective-permute-start(bf16[128,4096]{1,0:T(8,128)(2,1)S(1)} %collective-permute-done.10), channel_id=1, source_target_pairs={{0,2},{2,4},{4,6},{6,8},{8,10},{10,12},{12,14},{14,16},{16,18},{18... | collective-permute-start | bytes 3145736 | tf_op jit(solution)/shard_map/ppermute | solution.py:26
  230.6 47.7 %collective-permute-start.13 = (bf16[128,4096]{1,0:T(8,128)(2,1)S(1)}, bf16[128,4096]{1,0:T(8,128)(2,1)S(1)}, u32[]{:S(2)}, u32[]{:S(2)}) collective-permute-start(bf16[128,4096]{1,0:T(8,128)(2,1)S(1)} %collective-permute-done.11), channel_id=1, source_target_pairs={{0,30},{2,0},{4,2},{6,4},{8,6},{10,8},{12,10},{14,12},{16,14},{18,... | collective-permute-start | bytes 3145736 | tf_op jit(solution)/shard_map/ppermute | solution.py:29
  239.5 48.2 %collective-permute-start.14 = (bf16[128,4096]{1,0:T(8,128)(2,1)S(1)}, bf16[128,4096]{1,0:T(8,128)(2,1)S(1)}, u32[]{:S(2)}, u32[]{:S(2)}) collective-permute-start(bf16[128,4096]{1,0:T(8,128)(2,1)S(1)} %collective-permute-done.12), channel_id=1, source_target_pairs={{0,2},{2,4},{4,6},{6,8},{8,10},{10,12},{12,14},{14,16},{16,18},{18... | collective-permute-start | bytes 3145736 | tf_op jit(solution)/shard_map/ppermute | solution.py:26
  332.7 6.3 copy-start.32
  332.7 6.3 copy-start.34
  340.6 8.7 copy-start.17
  340.7 8.7 copy-start.19
  340.7 8.6 copy-start.21
  340.7 8.6 copy-start.23
  349.3 9.1 copy-start.7
  358.4 8.6 copy-start.50
  372.6 14.7 slice-start
  372.6 14.7 slice-start.1
  372.6 15.8 slice-start.2
  372.6 17.0 slice-start.3
  400.2 10.0 copy-start.14
  400.2 10.0 copy-start.18
  400.2 10.0 copy-start.20
  400.2 332.9 %reduce-scatter.9.cloned.1.call-start = ((), (), s32[]{:S(2)}) async-start(), calls=%async_computation.13 | async-start | bytes 6291456 | tf_op jit(solution)/shard_map/reduce_scatter | solution.py:224
  415.2 6.4 copy-start.33
  415.2 6.4 copy-start.35
  436.4 18.7 %copy-start.10 = (bf16[512,2048]{1,0:T(8,128)(2,1)S(1)}, bf16[512,2048]{1,0:T(8,128)(2,1)}, u32[]{:S(2)}) copy-start(bf16[512,2048]{1,0:T(8,128)(2,1)} %all-gather.9.cloned.1.call-done) | copy-start | bytes 6291460
  585.6 217.9 %reduce-scatter.7.cloned.1.call-start = ((), (), s32[]{:S(2)}) async-start(), calls=%async_computation.10 | async-start | bytes 6291456 | tf_op jit(solution)/shard_map/reduce_scatter | solution.py:165
  611.7 426.0 %reduce-scatter.11.cloned.1.call-start = ((), (), s32[]{:S(2)}) async-start(), calls=%async_computation.14 | async-start | bytes 26738688 | tf_op jit(solution)/shard_map/reduce_scatter | solution.py:239
  625.4 749.1 %reduce-scatter.15.cloned.1.call-start = ((), (), s32[]{:S(2)}) async-start(), calls=%async_computation.16 | async-start | bytes 35651584 | tf_op jit(solution)/shard_map/reduce_scatter | solution.py:241
  643.4 1067.6 %reduce-scatter.17.cloned.1.call-start = ((), (), s32[]{:S(2)}) async-start(), calls=%async_computation.17 | async-start | bytes 35651584 | tf_op jit(solution)/shard_map/reduce_scatter | solution.py:242
  673.1 60.0 %copy-start.1 = (bf16[256,2048]{1,0:T(8,128)(2,1)S(1)}, bf16[256,2048]{1,0:T(8,128)(2,1)}, u32[]{:S(2)}) copy-start(bf16[256,2048]{1,0:T(8,128)(2,1)} %param.20) | copy-start | bytes 3145732
  673.1 60.0 %copy-start.37 = (f32[16,1,128]{2,1,0:T(1,128)S(1)}, f32[16,1,128]{2,1,0:T(1,128)}, u32[]{:S(2)}) copy-start(f32[16,1,128]{2,1,0:T(1,128)} %copy-done.36) | copy-start | bytes 24580
  673.1 60.0 %copy-start.39 = (f32[256]{0:T(256)S(1)}, f32[256]{0:T(256)}, u32[]{:S(2)}) copy-start(f32[256]{0:T(256)} %copy-done.38) | copy-start | bytes 3076
  673.1 60.0 %copy-start.41 = (f32[256]{0:T(256)S(1)}, f32[256]{0:T(256)}, u32[]{:S(2)}) copy-start(f32[256]{0:T(256)} %copy-done.40) | copy-start | bytes 3076
  676.8 7.6 copy-start.15
  681.3 121.1 %copy-start.42 = (bf16[128]{0:T(256)(128)(2,1)S(1)}, bf16[128]{0:T(256)(128)(2,1)}, u32[]{:S(2)}) copy-start(bf16[128]{0:T(256)(128)(2,1)} %param.21) | copy-start | bytes 772
  681.3 121.1 %copy-start.44 = (f32[128]{0:T(128)S(1)}, f32[128]{0:T(128)}, u32[]{:S(2)}) copy-start(f32[128]{0:T(128)} %param.28) | copy-start | bytes 1540
  681.3 121.1 %copy-start.45 = (f32[128]{0:T(128)S(1)}, f32[128]{0:T(128)}, u32[]{:S(2)}) copy-start(f32[128]{0:T(128)} %param.29) | copy-start | bytes 1540
  681.3 121.7 %copy-start.43 = (bf16[128]{0:T(256)(128)(2,1)S(1)}, bf16[128]{0:T(256)(128)(2,1)}, u32[]{:S(2)}) copy-start(bf16[128]{0:T(256)(128)(2,1)} %param.22) | copy-start | bytes 772
  681.3 121.7 %copy-start.46 = (f32[128]{0:T(128)S(1)}, f32[128]{0:T(128)}, u32[]{:S(2)}) copy-start(f32[128]{0:T(128)} %param.30) | copy-start | bytes 1540
  681.3 121.7 %copy-start.47 = (f32[128]{0:T(128)S(1)}, f32[128]{0:T(128)}, u32[]{:S(2)}) copy-start(f32[128]{0:T(128)} %param.31) | copy-start | bytes 1540
  733.1 70.4 %copy-start.4 = (f32[256,2048]{1,0:T(8,128)S(1)}, f32[256,2048]{1,0:T(8,128)}, u32[]{:S(2)}) copy-start(f32[256,2048]{1,0:T(8,128)} %reduce-scatter.9.cloned.1.call-done) | copy-start | bytes 6291460
  802.4 6.6 copy-start.48
  802.4 6.6 copy-start.49
  1044.8 6.3 copy-start.6
  1047.9 326.5 %copy-start.3 = (bf16[128,4096]{1,0:T(8,128)(2,1)S(1)}, bf16[128,4096]{1,0:T(8,128)(2,1)}, u32[]{:S(2)}) copy-start(bf16[128,4096]{1,0:T(8,128)(2,1)} %param.25) | copy-start | bytes 3145732
  1052.7 658.3 %copy-start.8 = (bf16[128,4096]{1,0:T(8,128)(2,1)S(1)}, bf16[128,4096]{1,0:T(8,128)(2,1)}, u32[]{:S(2)}) copy-start(bf16[128,4096]{1,0:T(8,128)(2,1)} %param.26) | copy-start | bytes 3145732
  (21 other events, 57.5 us)
Sparse Core Ops, SparseCore 0:
  9.6 35.7 all-gather.16
  47.6 83.2 all-gather.12
  133.0 35.0 all-gather.8
  170.1 144.8 all-gather.10
  317.1 125.4 all-gather.14
  444.6 125.0 all-gather.18
  573.7 102.9 reduce-scatter.12
  679.1 54.0 reduce-scatter.8
  735.5 54.3 reduce-scatter.6
  793.8 243.8 reduce-scatter.10
  1042.6 331.8 reduce-scatter.14
  1379.1 331.7 reduce-scatter.16
